TPU v7x, 32 devices: a whole 2x2x4 slice. The times are simulated.
32 devices in a mesh: ctx: 8 (over y, x, core), mp: 4 (over z).
Axes of the slice: x: 2, y: 2, z: 4, core: 2. Of those that a mesh axis runs over, the one named last changes fastest.
Arguments:
- queries: bfloat16 [128, 6144], P('ctx', 'mp'), may hold values from -9 to 9
- cache_keys: bfloat16 [8, 4096, 128], P('mp', 'ctx'), may hold values from -9 to 9, as said below
- cache_values: bfloat16 [8, 4096, 128], P('mp', 'ctx'), may hold values from -6 to 6, as said below
- new_keys: bfloat16 [8, 128, 128], P('mp', 'ctx'), may hold values from -6 to 6, as said below
- new_values: bfloat16 [8, 128, 128], P('mp', 'ctx'), may hold values from -6 to 6, as said below
- out_proj: bfloat16 [6144, 6144], P('mp', 'ctx'), may hold values from -3 to 3
- residual: bfloat16 [128, 6144], P('mp', 'ctx'), may hold values from -24 to 24
- norm_gain: bfloat16 [6144], replicated, may hold values from 0.5 to 1.5
- gate_proj: bfloat16 [8, 6144, 8192], P('ctx', None, 'mp'), may hold values from -0.078125 to 0.078125
- up_proj: bfloat16 [8, 6144, 8192], P('ctx', None, 'mp'), may hold values from -0.078125 to 0.078125
- down_proj: bfloat16 [8, 8192, 6144], P('ctx', 'mp'), may hold values from -0.09375 to 0.09375
- expert_ids: int32 [128, 2], replicated, may hold values from 0 to 7, all different within a row; in each aligned block of 128 rows (0 to 127, 128 to 255, ...) at most 64 rows name the same one
- route_logits: float32 [128, 2], replicated, may hold values from -6 to 6
Outputs:
- layer_out: bfloat16 [128, 6144], P('mp', 'ctx')
Inputs may be any that keep to these rules, and one draw needn't show every extreme that they name: `expert_ids`: each row names 2 different experts; at most 64 rows name one expert, a bound that some block reaches. `cache_keys`: slot s holds key head s * 1; slots of one key head are equal. `cache_values`: slot s holds value head s * 1; slots of one head are equal. `new_keys`: slot s holds key head s * 1; slots of one key head are equal. `new_values`: slot s holds value head s * 1; slots of one head are equal.
All inputs are finite; a program needn't handle non-finite values.
Results may differ from a plain program's by a relative error of at most 0.024.
Values may be sent and summed in bfloat16 or wider, within the bound.
No kernel may reach another device: no remote copies, remote signals or barrier semaphores. Data moves between devices by JAX's collectives and lax.ppermute only.
A program may use at most 128 MiB of HBM per device.

v0:
```python
import math
import jax
import jax.numpy as jnp
from jax import lax
from jax.sharding import PartitionSpec as P

D = 6144
EXPERTS = 8
TOP = 2
neg_big = -1e30
norm_eps = 1e-05


def route_slots(expert_ids):
    flat = expert_ids.reshape(-1)
    onehot = (flat[:, None] == jnp.arange(EXPERTS, dtype=jnp.int32)[None, :]).astype(jnp.int32)
    before = jnp.cumsum(onehot, axis=0, dtype=jnp.int32) - onehot
    return jnp.sum(before * onehot, axis=1, dtype=jnp.int32).reshape(expert_ids.shape)


def softmax_pieces(query_block, keys_local, values_local, allowed, scale):
    scores = (
        jnp.einsum("srd,skd->srk", query_block, keys_local, preferred_element_type=jnp.float32)
        * scale
    )
    scores = jnp.where(allowed[None, :, :], scores, neg_big)
    highest = jnp.max(scores, axis=2)
    expo = jnp.exp(scores - highest[:, :, None])
    denom = jnp.sum(expo, axis=2)
    summed = jnp.einsum(
        "srk,skd->srd", expo.astype(jnp.bfloat16), values_local, preferred_element_type=jnp.float32
    )
    return (highest, denom, summed)


def join_softmax(former, latter):
    highest = jnp.maximum(former[0], latter[0])
    right = jnp.exp(latter[0] - highest)
    denom = latter[1] * right
    summed = latter[2] * right[:, :, None]
    return (highest, denom, summed)


def on_device(
    queries,
    cache_keys,
    cache_values,
    new_keys,
    new_values,
    out_proj,
    residual,
    norm_gain,
    gate_proj,
    up_proj,
    down_proj,
    expert_ids,
    route_logits,
):
    ctx_count = lax.axis_size("ctx")
    mp_count = lax.axis_size("mp")
    ctx_index = lax.axis_index("ctx")
    mp_index = lax.axis_index("mp")
    tok_local = queries.shape[0]
    tokens = tok_local * ctx_count
    slot_local = cache_keys.shape[0]
    cache_local = cache_keys.shape[1]
    head_dim = cache_keys.shape[2]
    heads_local = queries.shape[1] // head_dim
    group_size = heads_local // slot_local
    width = cache_local + tok_local
    scale = 1.0 / math.sqrt(head_dim)
    d_local = out_proj.shape[1]
    key_value = jnp.stack(
        [
            jnp.concatenate([cache_keys, new_keys], axis=1),
            jnp.concatenate([cache_values, new_values], axis=1),
        ]
    )
    shaped = queries.reshape(tok_local, slot_local, group_size, head_dim)
    query_block = jnp.transpose(shaped, (1, 2, 0, 3)).reshape(
        slot_local, group_size * tok_local, head_dim
    )
    query_tok = ctx_index * tok_local + jnp.tile(jnp.arange(tok_local, dtype=jnp.int32), group_size)
    query_count = group_size * tok_local
    start_state = (
        jnp.full((slot_local, query_count), neg_big, jnp.float32),
        jnp.zeros((slot_local, query_count), jnp.float32),
        jnp.zeros((slot_local, query_count, head_dim), jnp.float32),
    )
    piece = lax.all_gather(key_value, "ctx", axis=2, tiled=True)
    position = jnp.arange(piece.shape[2], dtype=jnp.int32)
    shard = position // width
    within = position % width
    new_tok = shard * tok_local + within - cache_local
    allowed = (within[None, :] < cache_local) | (new_tok[None, :] <= query_tok[:, None])
    highest, denom, summed = join_softmax(
        start_state, softmax_pieces(query_block, piece[0], piece[1], allowed, scale)
    )
    shaped = (
        (summed / denom[:, :, None])
        .astype(jnp.bfloat16)
        .reshape(slot_local, group_size, tok_local, head_dim)
    )
    attn = jnp.transpose(shaped, (2, 0, 1, 3)).reshape(tok_local, heads_local * head_dim)
    projected = jnp.dot(
        lax.all_gather(attn, "ctx", axis=0, tiled=True),
        out_proj,
        preferred_element_type=jnp.float32,
    )
    res_rows = residual.shape[0]
    res_start = mp_index * res_rows
    current = lax.dynamic_slice_in_dim(projected, res_start, res_rows, 0)
    projected = lax.dynamic_update_slice_in_dim(
        projected, current + residual.astype(jnp.float32), res_start, 0
    )
    hidden = lax.psum(projected.astype(jnp.bfloat16), "mp")
    capacity = tokens * TOP // 4
    slots = route_slots(expert_ids)
    per_row = max(1, EXPERTS // mp_count)
    first_expert = mp_index * EXPERTS // mp_count
    own_expert = (mp_index * ctx_count + ctx_index) * EXPERTS // (ctx_count * mp_count)
    local = own_expert - first_expert
    row_experts = first_expert + jnp.arange(per_row, dtype=jnp.int32)
    match = expert_ids[None, :, :] == row_experts[:, None, None]
    place = jnp.where(match, slots[None, :, :], capacity)
    table = place[:, :, :, None] == jnp.arange(capacity, dtype=jnp.int32)[None, None, None, :]
    pick = jnp.any(table, axis=2)
    packed = jnp.einsum(
        "rtc,td->rcd", pick.astype(jnp.bfloat16), hidden, preferred_element_type=jnp.float32
    ).astype(jnp.bfloat16)
    gate_local = gate_proj[0]
    up_local = up_proj[0]
    down_local = down_proj[0]
    chosen = lax.dynamic_index_in_dim(
        lax.all_gather(packed, "ctx", axis=2, tiled=True), local, 0, keepdims=False
    )
    wide = chosen.astype(jnp.float32)
    gains = norm_gain.astype(jnp.float32)
    scaled = (wide * gains[None, :]).astype(jnp.bfloat16)
    gate_sum = jnp.dot(scaled, gate_local, preferred_element_type=jnp.float32)
    up_sum = jnp.dot(scaled, up_local, preferred_element_type=jnp.float32)
    gate_sum, up_sum, squares = (gate_sum, up_sum, jnp.sum(wide * wide, axis=1))
    rms = lax.rsqrt(squares / D + norm_eps)
    act = (jax.nn.silu(rms[:, None] * gate_sum) * (rms[:, None] * up_sum)).astype(jnp.bfloat16)
    part = lax.dot_general(
        down_local, act, (((0,), (1,)), ((), ())), preferred_element_type=jnp.float32
    )
    returned = lax.psum_scatter(
        jnp.concatenate(
            [jnp.where(local == which, part, 0.0) for which in range(per_row)], axis=1
        ).astype(jnp.bfloat16),
        "ctx",
        scatter_dimension=0,
        tiled=True,
    ).astype(jnp.float32)
    weights = jax.nn.softmax(route_logits, axis=1)
    combine = jnp.sum(jnp.where(table, weights[None, :, :, None], 0.0), axis=2)
    moe = jnp.einsum(
        "drc,rtc->td",
        returned.reshape(d_local, per_row, capacity),
        combine,
        precision=lax.Precision.HIGHEST,
        preferred_element_type=jnp.float32,
    )
    share = lax.psum_scatter(
        moe.astype(jnp.bfloat16), "mp", scatter_dimension=0, tiled=True
    ).astype(jnp.float32)
    own_hidden = lax.dynamic_slice_in_dim(hidden, res_start, res_rows, 0).astype(jnp.float32)
    return (own_hidden + share).astype(jnp.bfloat16)


def solution(mesh):
    placed = (
        P("ctx", "mp"),
        P("mp", "ctx", None),
        P("mp", "ctx", None),
        P("mp", "ctx", None),
        P("mp", "ctx", None),
        P("mp", "ctx"),
        P("mp", "ctx"),
        P(),
        P("ctx", None, "mp"),
        P("ctx", None, "mp"),
        P("ctx", "mp", None),
        P(),
        P(),
    )
    return jax.shard_map(
        on_device, mesh=mesh, in_specs=placed, out_specs=P("mp", "ctx"), check_vma=False
    )
```

profile of v0, /device:TPU:0, one launch (start us, length us, event | category | flops | bytes accessed | tf_op | source)
XLA Modules:
  0.0 234.1 jit_solution(1601538211125830650)
XLA Ops:
  6.5 0.0 copy-start
  6.5 0.0 copy-start.2
  6.5 0.0 all-gather.3.cloned.1.call-start
  6.5 1.3 maximum_bitcast_fusion
  7.8 0.9 pad_maximum_fusion.1
  8.7 0.0 all-gather.3.cloned.1.call-update
  8.7 0.0 all-reduce.2.cloned.1.call-start
  8.8 0.8 copy.30
  9.5 0.1 eq.70
  9.7 0.1 eq.66
  9.8 0.6 reduce-window.6
  10.4 0.2 slice_reduce_fusion
  10.7 0.1 fusion.64
  10.8 0.1 broadcast_in_dim.67
  10.9 0.1 copy.32
  11.0 0.1 add.99
  11.1 0.0 copy-done.2
  11.1 0.1 reshape.149
  11.3 0.3 compare_or_fusion
  11.6 37.6 %all-gather.3.cloned.1.call-done = bf16[2,2,4224,128]{3,2,1,0:T(8,128)(2,1)} async-done(((bf16[2,2,528,128]{3,2,1,0:T(8,128)(2,1)}), bf16[2,2,4224,128]{3,2,1,0:T(8,128)(2,1)}) %all-gather.3.cloned.1.call-update) | async-done | bytes 4325392 | tf_op jit(solution)/shard_map/all_gather | solution.py:90
  49.3 0.0 slice-start
  49.3 0.0 slice-start.1
  49.3 2.8 %fusion.74 = (f32[2,96]{1,0:T(2,128)S(1)}, f32[2,96,4224]{2,1,0:T(8,128)S(1)}) fusion(bf16[2,96,128]{2,1,0:T(8,128)(2,1)S(1)} %bitcast.87, bf16[2,2,4224,128]{3,2,1,0:T(8,128)(2,1)} %all-gather.3.cloned.1.call-done, pred[96,4224]{1,0:T(8,128)(4,1)S(1)} %compare_or_fusion), kind=kOutput, calls=%fused_computation.88 | convolution fusion | flops 210050880 | bytes 5862144 | tf_op jit(solution)/shard_map/srd,skd->srk/dot_general | solution.py:23
  52.1 0.6 fusion.8
  52.7 0.0 slice-done
  52.7 0.0 slice-done.1
  52.7 0.8 fusion.36
  53.5 0.0 copy-start.3
  53.5 0.0 copy-start.6
  53.5 0.0 copy-start.4
  53.6 0.1 reshape.152
  53.7 9.6 %all_gather.10 = bf16[128,1536]{1,0:T(8,128)(2,1)S(1)} all-gather(bf16[16,1536]{1,0:T(8,128)(2,1)S(1)} %reshape.152), channel_id=1, replica_groups=mesh['ctx'=8,'mp'=4] {'ctx'}, dimensions={0}, use_global_device_ids=true | all-gather | bytes 442368 | tf_op jit(solution)/shard_map/all_gather | solution.py:106
  63.2 0.0 copy-done
  63.2 0.5 fusion.81
  63.7 0.0 copy-done.3
  63.7 0.7 convert_element_type.59
  64.4 0.0 all-reduce.2.cloned.1.call-update
  64.4 0.0 all-gather.5.cloned.1.call-start
  64.5 0.0 copy-done.6
  64.5 0.1 compare_select_fusion
  64.6 34.8 %all-reduce.2.cloned.1.call-done = bf16[128,768]{1,0:T(8,128)(2,1)} async-done(((bf16[128,768]{1,0:T(8,128)(2,1)}), bf16[128,768]{1,0:T(8,128)(2,1)}) %all-reduce.2.cloned.1.call-update) | async-done | bytes 196624 | tf_op jit(solution)/shard_map/psum | solution.py:116
  99.5 1.8 convolution_convert_fusion
  101.2 0.0 all-gather.5.cloned.1.call-update
  101.3 0.2 reduce-scatter.3.cloned.1.call-start
  101.5 0.0 copy-done.4
  101.6 25.4 %all-gather.5.cloned.1.call-done = bf16[2,64,6144]{2,1,0:T(8,128)(2,1)} async-done(((bf16[2,64,768]{2,1,0:T(8,128)(2,1)}), bf16[2,64,6144]{2,1,0:T(8,128)(2,1)}) %all-gather.5.cloned.1.call-update) | async-done | bytes 1572880 | tf_op jit(solution)/shard_map/all_gather | solution.py:135
  127.0 1.4 fusion.27
  128.4 13.7 %fusion.10 = f32[64,2048]{1,0:T(8,128)} fusion(bf16[1,6144,2048]{2,1,0:T(8,128)(2,1)} %param.21, f32[6144]{0:T(1024)S(1)} %convert_element_type.65, bf16[2,64,6144]{2,1,0:T(8,128)(2,1)} %all-gather.5.cloned.1.call-done, s32[]{:T(128)S(6)} %select_n.86, f32[64]{0:T(128)S(1)} %add_rsqrt_fusion), kind=kOutput, calls=%fused_computation.12 | convolution fusion | flops 1611923456 | bytes 26501380 | tf_op jit(solution)/shard_map/dot_general | solution.py:140
  142.1 0.0 copy-start.1
  142.1 21.4 %fusion.39 = (bf16[6144,64]{0,1:T(8,128)(2,1)S(1)}, bf16[6144,64]{0,1:T(8,128)(2,1)}) fusion(pred[]{:T(512)S(6)} %eq.77, pred[]{:T(512)S(6)} %eq.78, bf16[1,2048,6144]{2,1,0:T(8,128)(2,1)} %param.23, bf16[1,6144,2048]{2,1,0:T(8,128)(2,1)} %param.22, f32[6144]{0:T(1024)S(1)} %convert_element_type.65, bf16[2,64,6144]{2,1,0:T(8,128)(2,1)} %all-gather.5.cloned.1.call-done, ...), kind=kOutput, calls=%fused_computation.34 | convolution fusion | flops 3224109056 | bytes 53240072 | tf_op jit(solution)/shard_map/dot_general | solution.py:145
  163.5 0.0 copy-start.5
  163.5 2.4 %pad_maximum_fusion = bf16[6144,128]{0,1:T(8,128)(2,1)} fusion(bf16[6144,64]{0,1:T(8,128)(2,1)} %get-tuple-element.6, bf16[6144,64]{0,1:T(8,128)(2,1)S(1)} %get-tuple-element.5), kind=kLoop, calls=%fused_computation.25 | loop fusion | flops 3145728 | bytes 3145728 | tf_op jit(solution)/shard_map/concatenate | solution.py:149
  165.9 0.0 reduce-scatter.3.cloned.1.call-update
  166.0 0.0 reduce-scatter.5.cloned.1.call-start
  166.0 0.0 copy-done.5
  166.1 38.5 %reduce-scatter.3.cloned.1.call-done = bf16[768,128]{0,1:T(8,128)(2,1)} async-done(((bf16[6144,128]{0,1:T(8,128)(2,1)}), bf16[768,128]{0,1:T(8,128)(2,1)}) %reduce-scatter.3.cloned.1.call-update) | async-done | bytes 196624 | tf_op jit(solution)/shard_map/reduce_scatter | solution.py:148
  204.6 2.0 fusion.29
  206.5 0.0 reduce-scatter.5.cloned.1.call-update
  206.6 19.6 %reduce-scatter.5.cloned.1.call-done = bf16[32,768]{1,0:T(8,128)(2,1)} async-done(((bf16[128,768]{1,0:T(8,128)(2,1)}), bf16[32,768]{1,0:T(8,128)(2,1)}) %reduce-scatter.5.cloned.1.call-update) | async-done | bytes 49168 | tf_op jit(solution)/shard_map/reduce_scatter | solution.py:165
  226.1 1.5 add_convert_fusion
  227.6 0.0 copy-done.1
  (19 shorter events, 0.3 us)
Async XLA Ops:
  6.5 56.7 %copy-start = (bf16[1536,768]{1,0:T(8,128)(2,1)S(1)}, bf16[1536,768]{1,0:T(8,128)(2,1)}, u32[]{:S(2)}) copy-start(bf16[1536,768]{1,0:T(8,128)(2,1)} %param.18) | copy-start | bytes 7077892
  6.5 4.6 %copy-start.2 = (bf16[16,1536]{1,0:T(8,128)(2,1)S(1)}, bf16[16,1536]{1,0:T(8,128)(2,1)}, u32[]{:S(2)}) copy-start(bf16[16,1536]{1,0:T(8,128)(2,1)} %param.13) | copy-start | bytes 147460
  6.5 42.7 %all-gather.3.cloned.1.call-start = ((), (), s32[]{:S(2)}) async-start(), calls=%async_computation.2 | async-start | bytes 4866048 | tf_op jit(solution)/shard_map/all_gather | solution.py:90
  8.7 90.8 %all-reduce.2.cloned.1.call-start = ((), (), s32[]{:S(2)}) async-start(), calls=%async_computation.3 | async-start | bytes 393216 | tf_op jit(solution)/shard_map/psum | solution.py:116
  49.3 3.4 %slice-start = ((s8[4325376]{0:T(1024)(128)(4,1)}), s8[4194304]{0:T(1024)(128)(4,1)S(1)}, s32[]{:S(2)}) async-start(s8[4325376]{0:T(1024)(128)(4,1)} %bitcast.89), calls=%async_computation.7 | async-start | bytes 8388608
  49.3 3.4 %slice-start.1 = ((s8[4325376]{0:T(1024)(128)(4,1)}), s8[131072]{0:T(1024)(128)(4,1)S(1)}, s32[]{:S(2)}) async-start(s8[4325376]{0:T(1024)(128)(4,1)} %bitcast.89), calls=%async_computation.8 | async-start | bytes 262144
  53.5 10.2 %copy-start.3 = (bf16[32,768]{1,0:T(8,128)(2,1)S(1)}, bf16[32,768]{1,0:T(8,128)(2,1)}, u32[]{:S(2)}) copy-start(bf16[32,768]{1,0:T(8,128)(2,1)} %param.19) | copy-start | bytes 147460
  53.5 11.0 %copy-start.6 = (s32[128,2]{0,1:T(2,128)S(1)}, s32[128,2]{0,1:T(2,128)}, u32[]{:S(2)}) copy-start(s32[128,2]{0,1:T(2,128)} %param.24) | copy-start | bytes 3076
  53.5 48.0 %copy-start.4 = (bf16[6144]{0:T(1024)(128)(2,1)S(1)}, bf16[6144]{0:T(1024)(128)(2,1)}, u32[]{:S(2)}) copy-start(bf16[6144]{0:T(1024)(128)(2,1)} %param.20) | copy-start | bytes 36868
  64.4 62.5 %all-gather.5.cloned.1.call-start = ((), (), s32[]{:S(2)}) async-start(), calls=%async_computation.4 | async-start | bytes 1769472 | tf_op jit(solution)/shard_map/all_gather | solution.py:135
  101.3 103.3 %reduce-scatter.3.cloned.1.call-start = ((), (), s32[]{:S(2)}) async-start(), calls=%async_computation.5 | async-start | bytes 1769472 | tf_op jit(solution)/shard_map/reduce_scatter | solution.py:148
  142.1 85.5 %copy-start.1 = (bf16[1536,768]{1,0:T(8,128)(2,1)S(1)}, bf16[1536,768]{1,0:T(8,128)(2,1)}, u32[]{:S(2)}) copy-start(bf16[1536,768]{1,0:T(8,128)(2,1)} %param.18) | copy-start | bytes 7077892
  163.5 2.5 %copy-start.5 = (f32[128,2]{0,1:T(2,128)S(1)}, f32[128,2]{0,1:T(2,128)}, u32[]{:S(2)}) copy-start(f32[128,2]{0,1:T(2,128)} %param.25) | copy-start | bytes 3076
  166.0 60.2 %reduce-scatter.5.cloned.1.call-start = ((), (), s32[]{:S(2)}) async-start(), calls=%async_computation.6 | async-start | bytes 245760 | tf_op jit(solution)/shard_map/reduce_scatter | solution.py:165
Sparse Core Ops, SparseCore 0:
  9.3 39.9 all-gather.2
  64.6 34.8 all-reduce.1
  101.5 25.3 all-gather.4
  166.1 38.4 reduce-scatter.2
  206.8 19.3 reduce-scatter.4
where the time goes:
time: 235 us; the launch traced here: 234 us
  waiting for transfers between devices  156 us (66%)
  matrix products  42.9 us (18%)
  between operations  13.4 us (6%)
  other arithmetic  10 us (4%)
  blocking collectives  9.55 us (4%)
    reduce_scatter x1, waiting for transfers between devices, on_device(): lax.psum_scatter(jnp.concatenate([jnp.where(local == which, part, 0.0) fo...  38.5 us
    all_gather x1, waiting for transfers between devices, on_device(): piece = lax.all_gather(key_value, 'ctx', axis=2, tiled=True)  37.6 us
    psum x1, waiting for transfers between devices, on_device(): hidden = lax.psum(projected.astype(jnp.bfloat16), 'mp')  34.8 us
    all_gather x1, waiting for transfers between devices, on_device(): lax.all_gather(packed, 'ctx', axis=2, tiled=True)  25.4 us
    dot_general x1, matrix products, on_device(): lax.dot_general(down_local, act, (((0,), (1,)), ((), ())), preferred_elem...  21.4 us
    reduce_scatter x1, waiting for transfers between devices, on_device(): lax.psum_scatter(moe.astype(jnp.bfloat16), 'mp', scatter_dimension=0, til...  19.6 us
    dot_general x1, matrix products, on_device(): gate_sum = jnp.dot(scaled, gate_local, preferred_element_type=jnp.float32)  13.7 us
    all_gather x1, blocking collectives, on_device(): lax.all_gather(attn, 'ctx', axis=0, tiled=True)  9.55 us
  transfers between devices with their start and end apart: 5, of which 5 were waited for; matrix products, arithmetic and copies ran while one was open for 1% of the time, Pallas kernels for 0%

commit v1 on v0

--- a/solution.py
+++ b/solution.py
@@ -9,6 +9,19 @@
 TOP = 2
 neg_big = -1e30
 norm_eps = 1e-05
+
+
+def collect(shard, axis, dim):
+    ways = lax.axis_size(axis)
+    up = [(d, (d + 1) % ways) for d in range(ways)]
+    down = [(d, (d - 1) % ways) for d in range(ways)]
+    earlier, later = ([shard], [shard])
+    for _ in range(ways // 2):
+        earlier.append(lax.ppermute(earlier[-1], axis, up))
+    for _ in range((ways - 1) // 2):
+        later.append(lax.ppermute(later[-1], axis, down))
+    line = jnp.concatenate([*earlier[::-1], *later[1:]], axis=dim)
+    return jnp.roll(line, (lax.axis_index(axis) - ways // 2) * shard.shape[dim], axis=dim)
 
 
 def route_slots(expert_ids):
@@ -87,7 +100,7 @@
         jnp.zeros((slot_local, query_count), jnp.float32),
         jnp.zeros((slot_local, query_count, head_dim), jnp.float32),
     )
-    piece = lax.all_gather(key_value, "ctx", axis=2, tiled=True)
+    piece = collect(key_value, "ctx", 2)
     position = jnp.arange(piece.shape[2], dtype=jnp.int32)
     shard = position // width
     within = position % width

time: 235 us -> 263 us (1.12)
  local copies, waits for them, and re-layouts: 1.81 us -> 15.1 us
  starting transfers between devices: 0.35 us -> 8.91 us
  blocking collectives: 9.55 us -> 15.1 us
    ppermute x0 -> x7, waiting for transfers between devices: none -> 39.3 us  [the longest x4 39.1 us: collect(): earlier.append(lax.ppermute(earlier[-1], axis, up))]
    all_gather x1 -> x0, waiting for transfers between devices: 37.6 us -> none  [on_device(): piece = lax.all_gather(key_value, 'ctx', axis=2, tiled=True)]
    unnamed x19 -> x30, local copies, waits for them, and re-layouts: 0.83 us -> 13.2 us
    ppermute x0 -> x7, starting transfers between devices: none -> 8.6 us  [the longest x3 8.14 us: collect(): later.append(lax.ppermute(later[-1], axis, down))]
    all_gather x1, blocking collectives: 9.55 us -> 15.1 us  [on_device(): lax.all_gather(attn, 'ctx', axis=0, tiled=True)]
  transfers between devices with their start and end apart: 5 -> 11, of which waited for: 5 -> 9; matrix products, arithmetic and copies ran while one was open for 1% -> 4% of each run, Pallas kernels for 0% -> 0%
where the time goes in v1:
time: 263 us; the launch traced here: 262 us
  waiting for transfers between devices  158 us (60%)
  matrix products  42 us (16%)
  local copies, waits for them, and re-layouts  15.1 us (6%)
  blocking collectives  15.1 us (6%)
  between operations  13.5 us (5%)
  other arithmetic  10.1 us (4%)
  starting transfers between devices  8.91 us (3%)
    ppermute x4, waiting for transfers between devices, collect(): earlier.append(lax.ppermute(earlier[-1], axis, up))  39.1 us
    reduce_scatter x1, waiting for transfers between devices, on_device(): lax.psum_scatter(jnp.concatenate([jnp.where(local == which, part, 0.0) fo...  38.5 us
    psum x1, waiting for transfers between devices, on_device(): hidden = lax.psum(projected.astype(jnp.bfloat16), 'mp')  34.9 us
    all_gather x1, waiting for transfers between devices, on_device(): lax.all_gather(packed, 'ctx', axis=2, tiled=True)  25.4 us
    dot_general x1, matrix products, on_device(): lax.dot_general(down_local, act, (((0,), (1,)), ((), ())), preferred_elem...  21.4 us
    reduce_scatter x1, waiting for transfers between devices, on_device(): lax.psum_scatter(moe.astype(jnp.bfloat16), 'mp', scatter_dimension=0, til...  19.6 us
    all_gather x1, blocking collectives, on_device(): lax.all_gather(attn, 'ctx', axis=0, tiled=True)  15.1 us
    dot_general x1, matrix products, on_device(): gate_sum = jnp.dot(scaled, gate_local, preferred_element_type=jnp.float32)  13.7 us
  transfers between devices with their start and end apart: 11, of which 9 were waited for; matrix products, arithmetic and copies ran while one was open for 4% of the time, Pallas kernels for 0%

profile of v1, /device:TPU:0, one launch (start us, length us, event | category | flops | bytes accessed | tf_op | source)
XLA Modules:
  0.0 262.4 jit_solution(7812944390052913208)
XLA Ops:
  6.5 1.2 maximum_bitcast_fusion
  7.8 0.8 pad_maximum_fusion.1
  8.6 0.5 collective-permute-start
  9.1 10.1 %collective-permute-done = bf16[2,2,528,128]{3,2,1,0:T(8,128)(2,1)S(1)} collective-permute-done((bf16[2,2,528,128]{3,2,1,0:T(8,128)(2,1)}, bf16[2,2,528,128]{3,2,1,0:T(8,128)(2,1)S(1)}, u32[]{:S(2)}, u32[]{:S(2)}) %collective-permute-start) | collective-permute-done | bytes 540704 | tf_op jit(solution)/shard_map/ppermute | solution.py:20
  19.2 2.6 %collective-permute-start.4 = (bf16[2,2,528,128]{3,2,1,0:T(8,128)(2,1)}, bf16[2,2,528,128]{3,2,1,0:T(8,128)(2,1)}, u32[]{:S(2)}, u32[]{:S(2)}) collective-permute-start(bf16[2,2,528,128]{3,2,1,0:T(8,128)(2,1)} %pad_maximum_fusion.1), channel_id=1, source_target_pairs={{0,28},{4,0},{8,4},{12,8},{16,12},{20,16},{24,20},{28,24},{1,29},{... | collective-permute-start | bytes 1622024 | tf_op jit(solution)/shard_map/ppermute | solution.py:22
  21.9 0.1 add.110
  22.0 10.8 %collective-permute-done.1 = bf16[2,2,528,128]{3,2,1,0:T(8,128)(2,1)} collective-permute-done((bf16[2,2,528,128]{3,2,1,0:T(8,128)(2,1)S(1)}, bf16[2,2,528,128]{3,2,1,0:T(8,128)(2,1)}, u32[]{:S(2)}, u32[]{:S(2)}) %collective-permute-start.1) | collective-permute-done | bytes 540704 | tf_op jit(solution)/shard_map/ppermute | solution.py:20
  32.8 0.3 compare_or_fusion
  33.2 0.8 copy.30
  34.0 0.1 eq.73
  34.1 0.1 eq.69
  34.3 0.9 reshape.149
  35.2 2.7 %collective-permute-start.5 = (bf16[2,2,528,128]{3,2,1,0:T(8,128)(2,1)}, bf16[2,2,528,128]{3,2,1,0:T(8,128)(2,1)}, u32[]{:S(2)}, u32[]{:S(2)}) collective-permute-start(bf16[2,2,528,128]{3,2,1,0:T(8,128)(2,1)} %collective-permute-done.4), channel_id=1, source_target_pairs={{0,28},{4,0},{8,4},{12,8},{16,12},{20,16},{24,20},{28,24},{1,29},{... | collective-permute-start | bytes 1622024 | tf_op jit(solution)/shard_map/ppermute | solution.py:22
  37.9 8.4 %collective-permute-done.2 = bf16[2,2,528,128]{3,2,1,0:T(8,128)(2,1)} collective-permute-done((bf16[2,2,528,128]{3,2,1,0:T(8,128)(2,1)}, bf16[2,2,528,128]{3,2,1,0:T(8,128)(2,1)}, u32[]{:S(2)}, u32[]{:S(2)}) %collective-permute-start.2) | collective-permute-done | bytes 540704 | tf_op jit(solution)/shard_map/ppermute | solution.py:20
  46.3 0.6 reduce-window.6
  46.8 0.2 slice_reduce_fusion
  47.1 0.1 fusion.64
  47.2 0.1 broadcast_in_dim.67
  47.3 0.1 copy.32
  47.4 0.2 collective-permute-done.5
  47.6 2.8 %collective-permute-start.6 = (bf16[2,2,528,128]{3,2,1,0:T(8,128)(2,1)}, bf16[2,2,528,128]{3,2,1,0:T(8,128)(2,1)S(1)}, u32[]{:S(2)}, u32[]{:S(2)}) collective-permute-start(bf16[2,2,528,128]{3,2,1,0:T(8,128)(2,1)} %collective-permute-done.5), channel_id=1, source_target_pairs={{0,28},{4,0},{8,4},{12,8},{16,12},{20,16},{24,20},{28,24},{1,29},{... | collective-permute-start | bytes 1622024 | tf_op jit(solution)/shard_map/ppermute | solution.py:22
  50.4 9.8 %collective-permute-done.3 = bf16[2,2,528,128]{3,2,1,0:T(8,128)(2,1)} collective-permute-done((bf16[2,2,528,128]{3,2,1,0:T(8,128)(2,1)}, bf16[2,2,528,128]{3,2,1,0:T(8,128)(2,1)}, u32[]{:S(2)}, u32[]{:S(2)}) %collective-permute-start.3) | collective-permute-done | bytes 540704 | tf_op jit(solution)/shard_map/ppermute | solution.py:20
  60.2 1.1 constant_dynamic-update-slice_fusion.15
  61.3 1.1 constant_dynamic-update-slice_fusion.14
  62.4 1.1 constant_dynamic-update-slice_fusion.13
  63.5 1.1 constant_dynamic-update-slice_fusion.12
  64.7 0.1 constant_dynamic-update-slice_fusion.11
  64.8 1.1 constant_dynamic-update-slice_fusion.10
  65.9 1.1 constant_dynamic-update-slice_fusion.9
  67.0 0.1 constant_dynamic-update-slice_fusion.8
  67.1 1.1 constant_dynamic-update-slice_fusion.7
  68.2 1.1 constant_dynamic-update-slice_fusion.6
  69.3 1.1 constant_dynamic-update-slice_fusion.5
  70.5 0.1 constant_dynamic-update-slice_fusion.4
  70.5 0.1 constant_dynamic-update-slice_fusion.3
  70.6 1.1 constant_dynamic-update-slice_fusion.2
  71.7 1.1 constant_dynamic-update-slice_fusion.1
  72.9 0.1 constant_dynamic-update-slice_fusion
  73.0 1.5 fusion.76
  74.5 0.6 fusion.8
  75.1 1.2 fusion.36
  76.3 0.1 reshape.152
  76.4 15.1 %all_gather.6 = bf16[128,1536]{1,0:T(8,128)(2,1)S(1)} all-gather(bf16[16,1536]{1,0:T(8,128)(2,1)S(1)} %reshape.152), channel_id=1, replica_groups=mesh['ctx'=8,'mp'=4] {'ctx'}, dimensions={0}, use_global_device_ids=true | all-gather | bytes 442368 | tf_op jit(solution)/shard_map/all_gather | solution.py:119
  91.5 0.5 fusion.83
  92.1 0.7 convert_element_type.59
  92.8 0.0 all-reduce.2.cloned.1.call-update
  92.8 0.0 all-gather.2.cloned.1.call-start
  92.8 0.1 compare_select_fusion
  92.9 34.9 %all-reduce.2.cloned.1.call-done = bf16[128,768]{1,0:T(8,128)(2,1)} async-done(((bf16[128,768]{1,0:T(8,128)(2,1)}), bf16[128,768]{1,0:T(8,128)(2,1)}) %all-reduce.2.cloned.1.call-update) | async-done | bytes 196624 | tf_op jit(solution)/shard_map/psum | solution.py:129
  127.8 1.8 convolution_convert_fusion
  129.6 0.0 all-gather.2.cloned.1.call-update
  129.6 0.2 reduce-scatter.3.cloned.1.call-start
  129.9 25.4 %all-gather.2.cloned.1.call-done = bf16[2,64,6144]{2,1,0:T(8,128)(2,1)} async-done(((bf16[2,64,768]{2,1,0:T(8,128)(2,1)}), bf16[2,64,6144]{2,1,0:T(8,128)(2,1)}) %all-gather.2.cloned.1.call-update) | async-done | bytes 1572880 | tf_op jit(solution)/shard_map/all_gather | solution.py:148
  155.3 1.4 fusion.27
  156.7 13.7 %fusion.10 = f32[64,2048]{1,0:T(8,128)} fusion(bf16[1,6144,2048]{2,1,0:T(8,128)(2,1)} %param.21, f32[6144]{0:T(1024)S(1)} %convert_element_type.65, bf16[2,64,6144]{2,1,0:T(8,128)(2,1)} %all-gather.2.cloned.1.call-done, s32[]{:T(128)S(6)} %select_n.100, f32[64]{0:T(128)S(1)} %add_rsqrt_fusion), kind=kOutput, calls=%fused_computation.12 | convolution fusion | flops 1611923456 | bytes 26501380 | tf_op jit(solution)/shard_map/dot_general | solution.py:153
  170.4 21.4 %fusion.39 = (bf16[6144,64]{0,1:T(8,128)(2,1)S(1)}, bf16[6144,64]{0,1:T(8,128)(2,1)}) fusion(pred[]{:T(512)S(6)} %eq.80, pred[]{:T(512)S(6)} %eq.81, bf16[1,2048,6144]{2,1,0:T(8,128)(2,1)} %param.23, bf16[1,6144,2048]{2,1,0:T(8,128)(2,1)} %param.22, f32[6144]{0:T(1024)S(1)} %convert_element_type.65, bf16[2,64,6144]{2,1,0:T(8,128)(2,1)} %all-gather.2.cloned.1.call-done, ...), kind=kOutput, calls=%fused_computation.34 | convolution fusion | flops 3224109056 | bytes 53240072 | tf_op jit(solution)/shard_map/dot_general | solution.py:158
  191.8 2.4 pad_maximum_fusion
  194.2 0.0 reduce-scatter.3.cloned.1.call-update
  194.3 0.0 reduce-scatter.5.cloned.1.call-start
  194.4 38.5 %reduce-scatter.3.cloned.1.call-done = bf16[768,128]{0,1:T(8,128)(2,1)} async-done(((bf16[6144,128]{0,1:T(8,128)(2,1)}), bf16[768,128]{0,1:T(8,128)(2,1)}) %reduce-scatter.3.cloned.1.call-update) | async-done | bytes 196624 | tf_op jit(solution)/shard_map/reduce_scatter | solution.py:161
  232.9 2.0 fusion.29
  234.9 0.0 reduce-scatter.5.cloned.1.call-update
  234.9 19.6 %reduce-scatter.5.cloned.1.call-done = bf16[32,768]{1,0:T(8,128)(2,1)} async-done(((bf16[128,768]{1,0:T(8,128)(2,1)}), bf16[32,768]{1,0:T(8,128)(2,1)}) %reduce-scatter.5.cloned.1.call-update) | async-done | bytes 49168 | tf_op jit(solution)/shard_map/reduce_scatter | solution.py:178
  254.5 1.5 add_convert_fusion
  (40 shorter events, 0.3 us)
Async XLA Ops:
  6.5 85.0 %copy-start = (bf16[1536,768]{1,0:T(8,128)(2,1)S(1)}, bf16[1536,768]{1,0:T(8,128)(2,1)}, u32[]{:S(2)}) copy-start(bf16[1536,768]{1,0:T(8,128)(2,1)} %param.18) | copy-start | bytes 7077892
  6.5 121.2 %all-reduce.2.cloned.1.call-start = ((), (), s32[]{:S(2)}) async-start(), calls=%async_computation.2 | async-start | bytes 393216 | tf_op jit(solution)/shard_map/psum | solution.py:129
  8.6 10.6 %collective-permute-start = (bf16[2,2,528,128]{3,2,1,0:T(8,128)(2,1)}, bf16[2,2,528,128]{3,2,1,0:T(8,128)(2,1)S(1)}, u32[]{:S(2)}, u32[]{:S(2)}) collective-permute-start(bf16[2,2,528,128]{3,2,1,0:T(8,128)(2,1)} %pad_maximum_fusion.1), channel_id=1, source_target_pairs={{0,4},{4,8},{8,12},{12,16},{16,20},{20,24},{24,28},{28,0},{1,5},{5... | collective-permute-start | bytes 1622024 | tf_op jit(solution)/shard_map/ppermute | solution.py:20
  19.2 13.6 %copy-start.2 = (bf16[2,2,528,128]{3,2,1,0:T(8,128)(2,1)}, bf16[2,2,528,128]{3,2,1,0:T(8,128)(2,1)S(1)}, u32[]{:S(2)}) copy-start(bf16[2,2,528,128]{3,2,1,0:T(8,128)(2,1)S(1)} %collective-permute-done) | copy-start | bytes 1622020
  19.2 13.6 %collective-permute-start.1 = (bf16[2,2,528,128]{3,2,1,0:T(8,128)(2,1)S(1)}, bf16[2,2,528,128]{3,2,1,0:T(8,128)(2,1)}, u32[]{:S(2)}, u32[]{:S(2)}) collective-permute-start(bf16[2,2,528,128]{3,2,1,0:T(8,128)(2,1)S(1)} %collective-permute-done), channel_id=1, source_target_pairs={{0,4},{4,8},{8,12},{12,16},{16,20},{20,24},{24,28},{28,0},{1,5},{5... | collective-permute-start | bytes 1622024 | tf_op jit(solution)/shard_map/ppermute | solution.py:20
  19.2 16.0 %collective-permute-start.4 = (bf16[2,2,528,128]{3,2,1,0:T(8,128)(2,1)}, bf16[2,2,528,128]{3,2,1,0:T(8,128)(2,1)}, u32[]{:S(2)}, u32[]{:S(2)}) collective-permute-start(bf16[2,2,528,128]{3,2,1,0:T(8,128)(2,1)} %pad_maximum_fusion.1), channel_id=1, source_target_pairs={{0,28},{4,0},{8,4},{12,8},{16,12},{20,16},{24,20},{28,24},{1,29},{... | collective-permute-start | bytes 1622024 | tf_op jit(solution)/shard_map/ppermute | solution.py:22
  32.8 13.4 %collective-permute-start.2 = (bf16[2,2,528,128]{3,2,1,0:T(8,128)(2,1)}, bf16[2,2,528,128]{3,2,1,0:T(8,128)(2,1)}, u32[]{:S(2)}, u32[]{:S(2)}) collective-permute-start(bf16[2,2,528,128]{3,2,1,0:T(8,128)(2,1)} %collective-permute-done.1), channel_id=1, source_target_pairs={{0,4},{4,8},{8,12},{12,16},{16,20},{20,24},{24,28},{28,0},{1,5},{5... | collective-permute-start | bytes 1622024 | tf_op jit(solution)/shard_map/ppermute | solution.py:20
  35.2 12.4 %collective-permute-start.5 = (bf16[2,2,528,128]{3,2,1,0:T(8,128)(2,1)}, bf16[2,2,528,128]{3,2,1,0:T(8,128)(2,1)}, u32[]{:S(2)}, u32[]{:S(2)}) collective-permute-start(bf16[2,2,528,128]{3,2,1,0:T(8,128)(2,1)} %collective-permute-done.4), channel_id=1, source_target_pairs={{0,28},{4,0},{8,4},{12,8},{16,12},{20,16},{24,20},{28,24},{1,29},{... | collective-permute-start | bytes 1622024 | tf_op jit(solution)/shard_map/ppermute | solution.py:22
  46.3 14.0 %collective-permute-start.3 = (bf16[2,2,528,128]{3,2,1,0:T(8,128)(2,1)}, bf16[2,2,528,128]{3,2,1,0:T(8,128)(2,1)}, u32[]{:S(2)}, u32[]{:S(2)}) collective-permute-start(bf16[2,2,528,128]{3,2,1,0:T(8,128)(2,1)} %collective-permute-done.2), channel_id=1, source_target_pairs={{0,4},{4,8},{8,12},{12,16},{16,20},{20,24},{24,28},{28,0},{1,5},{5... | collective-permute-start | bytes 1622024 | tf_op jit(solution)/shard_map/ppermute | solution.py:20
  47.4 23.0 %copy-start.3 = (bf16[2,2,528,128]{3,2,1,0:T(8,128)(2,1)S(1)}, bf16[2,2,528,128]{3,2,1,0:T(8,128)(2,1)}, u32[]{:S(2)}) copy-start(bf16[2,2,528,128]{3,2,1,0:T(8,128)(2,1)} %copy-done.2) | copy-start | bytes 1622020
  47.6 19.4 %collective-permute-start.6 = (bf16[2,2,528,128]{3,2,1,0:T(8,128)(2,1)}, bf16[2,2,528,128]{3,2,1,0:T(8,128)(2,1)S(1)}, u32[]{:S(2)}, u32[]{:S(2)}) collective-permute-start(bf16[2,2,528,128]{3,2,1,0:T(8,128)(2,1)} %collective-permute-done.5), channel_id=1, source_target_pairs={{0,28},{4,0},{8,4},{12,8},{16,12},{20,16},{24,20},{28,24},{1,29},{... | collective-permute-start | bytes 1622024 | tf_op jit(solution)/shard_map/ppermute | solution.py:22
  72.9 19.1 %copy-start.4 = (bf16[32,768]{1,0:T(8,128)(2,1)S(1)}, bf16[32,768]{1,0:T(8,128)(2,1)}, u32[]{:S(2)}) copy-start(bf16[32,768]{1,0:T(8,128)(2,1)} %param.19) | copy-start | bytes 147460
  73.0 19.9 %copy-start.7 = (s32[128,2]{0,1:T(2,128)S(1)}, s32[128,2]{0,1:T(2,128)}, u32[]{:S(2)}) copy-start(s32[128,2]{0,1:T(2,128)} %param.24) | copy-start | bytes 3076
  74.5 55.4 %copy-start.5 = (bf16[6144]{0:T(1024)(128)(2,1)S(1)}, bf16[6144]{0:T(1024)(128)(2,1)}, u32[]{:S(2)}) copy-start(bf16[6144]{0:T(1024)(128)(2,1)} %param.20) | copy-start | bytes 36868
  92.8 62.5 %all-gather.2.cloned.1.call-start = ((), (), s32[]{:S(2)}) async-start(), calls=%async_computation.3 | async-start | bytes 1769472 | tf_op jit(solution)/shard_map/all_gather | solution.py:148
  129.6 103.3 %reduce-scatter.3.cloned.1.call-start = ((), (), s32[]{:S(2)}) async-start(), calls=%async_computation.4 | async-start | bytes 1769472 | tf_op jit(solution)/shard_map/reduce_scatter | solution.py:161
  170.4 23.9 %copy-start.6 = (f32[128,2]{0,1:T(2,128)S(1)}, f32[128,2]{0,1:T(2,128)}, u32[]{:S(2)}) copy-start(f32[128,2]{0,1:T(2,128)} %param.25) | copy-start | bytes 3076
  170.4 85.5 %copy-start.1 = (bf16[1536,768]{1,0:T(8,128)(2,1)S(1)}, bf16[1536,768]{1,0:T(8,128)(2,1)}, u32[]{:S(2)}) copy-start(bf16[1536,768]{1,0:T(8,128)(2,1)} %param.18) | copy-start | bytes 7077892
  194.3 60.2 %reduce-scatter.5.cloned.1.call-start = ((), (), s32[]{:S(2)}) async-start(), calls=%async_computation.5 | async-start | bytes 245760 | tf_op jit(solution)/shard_map/reduce_scatter | solution.py:178
Sparse Core Ops, SparseCore 0:
  92.9 34.8 all-reduce.1
  129.8 25.3 all-gather.1
  194.4 38.4 reduce-scatter.2
  235.1 19.3 reduce-scatter.4
